TPU v7x, 256 devices: a whole 4x4x8 slice. The times are simulated.
256 devices in a mesh: head: 4 (over x), page: 64 (over y, z, core).
Axes of the slice: x: 4, y: 4, z: 8, core: 2. Of those that a mesh axis runs over, the one named last changes fastest.
Arguments:
- hidden: bfloat16 [12, 2048], P(None, 'page'), may hold values from -6 to 6
- q_weight: bfloat16 [2048, 3072], P('page', 'head'), may hold values from -0.125 to 0.125
- key_up: bfloat16 [16, 128, 512], P('head'), may hold values from -0.5 to 0.5
- value_up_weight: bfloat16 [16, 512, 128], P('head'), may hold values from -0.25 to 0.25
- out_weight: bfloat16 [2048, 2048], P('head', 'page'), may hold values from -0.125 to 0.125
- cache: bfloat16 [16, 512, 128, 576], P('head', 'page'), may hold values from -360 to 360
- page_table: int32 [16, 512], P('head', 'page'), may hold values from 0 to 511, each once within a row
- seq_pages: int32 [12], replicated, may hold values from 1 to 128, 512 in all
- keep_rows: int32 [16, 512, 64], P('head'), may hold values from 0 to 127, as said below
- fold_mass: bfloat16 [16, 512, 64], P('head'), may hold values from 0.5 to 4
- new_place: int32 [16, 512], P('head'), may hold values from 0 to 2047, as said below
- norm_gain: bfloat16 [2048], replicated, may hold values from 0.099609375 to 1.8984375
- router: bfloat16 [2048, 64], replicated, may hold values from -0.125 to 0.125
- routes: int32 [12, 6], replicated, may hold values from 0 to 63, all different within a row
- w_gate: bfloat16 [64, 2048, 1408], P('page', None, 'head'), may hold values from -0.125 to 0.125
- w_up: bfloat16 [64, 2048, 1408], P('page', None, 'head'), may hold values from -0.125 to 0.125
- w_down: bfloat16 [64, 1408, 2048], P('page', 'head'), may hold values from -0.15625 to 0.15625
Outputs:
- attn_out: bfloat16 [12, 2048], replicated
- moe_out: bfloat16 [12, 2048], replicated
- new_rows: bfloat16 [8192, 64, 576], P(('head', 'page'))
- new_mass: bfloat16 [8192, 64], P(('head', 'page'))
Inputs may be any that keep to these rules, and one draw needn't show every extreme that they name: `keep_rows`: the 64 entries of each head and page are distinct. `new_place`: for each group of heads h // 4 the places form a permutation of 0 to 2047. Among the blocks of one head group whose pages share g // 8, at most 1 have places with the same place // 32, and some reach 1.
All inputs are finite; a program needn't handle non-finite values.
Results may differ from a plain program's by a relative error of at most 0.035.
Values may be sent and summed in bfloat16 or wider, within the bound.
A program may use at most 128 MiB of HBM per device.

v0:
```python
import jax
import jax.numpy as jnp
from jax import lax
from jax.sharding import PartitionSpec as P

QK_NOPE = 128
QK_ROPE = 64
THETA = 50000.0
ROUTE_SCALE = 2.446
NORM_EPS = 1e-06


def joined_2(part, axis, combine):
    gathered = jax.tree.map(lambda a: lax.all_gather(a, axis), part)

    def take(source):
        return jax.tree.map(lambda a: lax.dynamic_index_in_dim(a, source, 0, False), gathered)

    return lax.fori_loop(
        1, lax.axis_size(axis), lambda source, state: combine(state, take(source)), take(0)
    )


def rotate_query(values, positions):
    half_dim = values.shape[-1] // 2
    freqs = THETA ** (-2.0 * jnp.arange(half_dim, dtype=jnp.float32) / values.shape[-1])
    angles = positions.astype(jnp.float32)[:, None] * freqs[None, :]
    cosine = jnp.cos(angles)[:, None, :]
    sine_v = jnp.sin(angles)[:, None, :]
    front = values[..., :half_dim]
    back = values[..., half_dim:]
    return jnp.concatenate(
        [front * cosine - back * sine_v, back * cosine + front * sine_v], axis=-1
    )


def pick_rows(one_page, row_ids):
    return one_page[row_ids]


def merge_parts(left_part, right_part):
    joined = jnp.maximum(left_part[0], right_part[0])
    left_factor = jnp.exp(left_part[0] - joined)
    right_factor = jnp.exp(right_part[0] - joined)
    return (
        joined,
        left_part[1] * left_factor + right_part[1] * right_factor,
        left_part[2] * left_factor[..., None] + right_part[2] * right_factor[..., None],
    )


def shards(
    hidden,
    q_weight,
    key_up,
    value_up_weight,
    out_weight,
    cache,
    page_table,
    seq_pages,
    keep_rows,
    fold_mass,
    new_place,
    norm_gain,
    router,
    routes,
    w_gate,
    w_up,
    w_down,
):
    heads_here = key_up.shape[0]
    pages_here = cache.shape[1]
    page_rows = cache.shape[2]
    latent_dim = cache.shape[3]
    kv_rank = key_up.shape[2]
    kept_count = keep_rows.shape[2]
    requests = hidden.shape[0]
    head_size = QK_NOPE + QK_ROPE
    groups = lax.axis_size("page")
    page_index = lax.axis_index("page")
    blocks = heads_here * pages_here
    sending_limit = (blocks + groups - 1) // groups
    first_page = page_index * pages_here
    partial_value = jnp.dot(hidden, q_weight, preferred_element_type=jnp.float32)
    queries = lax.psum(partial_value, "page").reshape(requests, heads_here, head_size)
    q_nope = queries[..., :QK_NOPE].astype(jnp.bfloat16)
    positions = seq_pages * page_rows - 1
    q_rope = rotate_query(queries[..., QK_NOPE:], positions).astype(jnp.bfloat16)
    q_latent = jnp.einsum(
        "rhn,hnk->rhk", q_nope, key_up, preferred_element_type=jnp.float32
    ).astype(jnp.bfloat16)
    q_full = jnp.concatenate([q_latent, q_rope], axis=-1)
    keep_here = lax.dynamic_slice_in_dim(keep_rows, first_page, pages_here, 1)
    mass_here = lax.dynamic_slice_in_dim(fold_mass, first_page, pages_here, 1)
    compact = jax.vmap(jax.vmap(pick_rows))(cache, keep_here)
    flat_rows = compact.reshape(heads_here, pages_here * kept_count, latent_dim)
    page_ends = jnp.cumsum(seq_pages)
    owner = jnp.sum((page_table[..., None] >= page_ends).astype(jnp.int32), axis=-1)
    row_owner = jnp.repeat(owner, kept_count, axis=1)
    in_request = row_owner[:, None, :] == jnp.arange(requests, dtype=jnp.int32)[None, :, None]
    scores = jnp.einsum(
        "rhk,hnk->hrn", q_full, flat_rows, preferred_element_type=jnp.float32
    ) * head_size ** (-0.5)
    row_max = jnp.max(jnp.where(in_request, scores, -1e30), axis=-1)
    row_mass = mass_here.reshape(heads_here, 1, pages_here * kept_count).astype(jnp.float32)
    weights = jnp.where(in_request, row_mass * jnp.exp(scores - row_max[..., None]), 0.0)
    totals = jnp.sum(weights, axis=-1)
    weighted = jnp.einsum(
        "hrn,hnk->hrk",
        weights.astype(jnp.bfloat16),
        flat_rows[..., :kv_rank],
        preferred_element_type=jnp.float32,
    )
    best, mass_sum, latent_sum = joined_2((row_max, totals, weighted), "page", merge_parts)
    latent_output = (latent_sum / mass_sum[..., None]).astype(jnp.bfloat16)
    head_result_rows = jnp.einsum(
        "usj,ujb->sub", latent_output, value_up_weight, preferred_element_type=jnp.float32
    ).astype(jnp.bfloat16)
    head_result_rows = head_result_rows.reshape(requests, heads_here * value_up_weight.shape[2])
    out_cols = jnp.dot(head_result_rows, out_weight, preferred_element_type=jnp.float32)
    col_width = out_cols.shape[1]
    padded = jnp.zeros((requests, col_width * groups), jnp.float32)
    padded = lax.dynamic_update_slice_in_dim(padded, out_cols, page_index * col_width, 1)
    attn_out = lax.psum(padded, ("head", "page")).astype(jnp.bfloat16)
    attn_wide = attn_out.astype(jnp.float32)
    mean_sq = jnp.mean(attn_wide * attn_wide, axis=-1, keepdims=True)
    normed = (attn_wide * lax.rsqrt(mean_sq + NORM_EPS) * norm_gain.astype(jnp.float32)).astype(
        jnp.bfloat16
    )
    logits = jnp.dot(normed, router, preferred_element_type=jnp.float32)
    picked = jax.nn.sigmoid(jnp.take_along_axis(logits, routes, axis=1))
    shares = ROUTE_SCALE * picked / jnp.sum(picked, axis=1, keepdims=True)
    expert_ids = jnp.arange(logits.shape[1], dtype=jnp.int32)
    combine = jnp.sum(
        jnp.where(routes[:, :, None] == expert_ids[None, None, :], shares[:, :, None], 0.0), axis=1
    )
    local_experts = w_gate.shape[0]
    combine_here = lax.dynamic_slice_in_dim(combine, page_index * local_experts, local_experts, 1)
    gate_part = jnp.einsum("rd,edf->erf", normed, w_gate, preferred_element_type=jnp.float32)
    up_part = jnp.einsum("rd,edf->erf", normed, w_up, preferred_element_type=jnp.float32)
    expert_hidden = (jax.nn.silu(gate_part) * up_part).astype(jnp.bfloat16)
    expert_outs = jnp.einsum(
        "erf,efd->erd", expert_hidden, w_down, preferred_element_type=jnp.float32
    )
    expert_terms = jnp.sum(combine_here.T[:, :, None] * expert_outs, axis=0)
    moe_out = lax.psum(expert_terms, ("head", "page")).astype(jnp.bfloat16)
    dest_all = new_place // blocks
    slot_all = new_place % blocks
    dest_here = lax.dynamic_slice_in_dim(dest_all, first_page, pages_here, 1).reshape(blocks)
    peer_ids = jnp.arange(groups, dtype=jnp.int32)
    dest_onehot = (dest_here[:, None] == peer_ids[None, :]).astype(jnp.int32)
    send_rank = jnp.sum(jnp.cumsum(dest_onehot, axis=0) * dest_onehot, axis=1) - 1
    send_col = dest_here * sending_limit + send_rank
    slot_ids = jnp.arange(groups * sending_limit, dtype=jnp.int32)
    chooser = (send_col[:, None] == slot_ids[None, :]).astype(jnp.bfloat16)

    def arrange(values):
        return (
            values.reshape(heads_here, groups, pages_here)
            .transpose(1, 0, 2)
            .reshape(groups, blocks)
        )

    to_here = arrange(dest_all) == page_index
    recv_rank = jnp.cumsum(to_here.astype(jnp.int32), axis=1) - 1
    recv_col = peer_ids[:, None] * sending_limit + recv_rank
    block_ids = jnp.arange(blocks, dtype=jnp.int32)
    by_slot = ((arrange(slot_all)[..., None] == block_ids) & to_here[..., None]).astype(
        jnp.bfloat16
    )
    by_col = (recv_col[..., None] == slot_ids).astype(jnp.bfloat16)
    unpack = jnp.einsum("sbq,sbc->qc", by_slot, by_col, preferred_element_type=jnp.float32).astype(
        jnp.bfloat16
    )
    owned = (slot_all.reshape(-1)[None, :] == block_ids[:, None]) & (
        dest_all.reshape(-1)[None, :] == page_index
    )
    new_mass = jnp.dot(
        owned.astype(jnp.bfloat16),
        fold_mass.reshape(-1, kept_count),
        preferred_element_type=jnp.float32,
    ).astype(jnp.bfloat16)
    payload = cache.reshape(blocks, page_rows * latent_dim)
    outgoing = jnp.einsum("bc,bx->cx", chooser, payload, preferred_element_type=jnp.float32).astype(
        jnp.bfloat16
    )
    arrived_rows = lax.all_to_all(
        outgoing.reshape(groups, sending_limit, page_rows, latent_dim),
        "page",
        split_axis=0,
        concat_axis=0,
        tiled=True,
    )
    placed = jnp.dot(
        unpack,
        arrived_rows.reshape(groups * sending_limit, page_rows * latent_dim),
        preferred_element_type=jnp.float32,
    ).astype(jnp.bfloat16)
    keep_new = jnp.dot(owned.astype(jnp.int32), keep_rows.reshape(-1, kept_count))
    new_rows = jax.vmap(pick_rows)(placed.reshape(blocks, page_rows, latent_dim), keep_new)
    return (attn_out, moe_out, new_rows, new_mass)


def solution(mesh):
    in_specs = (
        P(None, "page"),
        P("page", "head"),
        P("head", None, None),
        P("head", None, None),
        P("head", "page"),
        P("head", "page", None, None),
        P("head", "page"),
        P(),
        P("head", None, None),
        P("head", None, None),
        P("head", None),
        P(),
        P(),
        P(),
        P("page", None, "head"),
        P("page", None, "head"),
        P("page", "head", None),
    )
    out_specs = (P(), P(), P(("head", "page"), None, None), P(("head", "page"), None))
    return jax.shard_map(shards, mesh=mesh, in_specs=in_specs, out_specs=out_specs, check_vma=False)
```

profile of v0, /device:TPU:1, one launch (start us, length us, event | category | flops | bytes accessed | tf_op | source)
XLA Modules:
  0.0 994.9 jit_solution(4305672104055780673)
XLA Ops:
  7.3 1.1 constant_dynamic-slice_fusion.2
  8.6 7.8 copy.109
  16.6 249.7 %psum.21 = f32[12,4,192]{2,0,1:T(8,128)S(1)} all-reduce(f32[12,4,192]{2,0,1:T(8,128)S(1)} %copy.107), channel_id=1, replica_groups=mesh['head'=4,'page'=64] {'page'}, use_global_device_ids=true, to_apply=%region_2.3 | all-reduce | flops 9216 | bytes 73728 | tf_op jit(solution)/shard_map/psum | solution.py:85
  267.1 39.7 %gather_fusion = bf16[2048,576]{1,0:T(8,128)(2,1)} fusion(bf16[4,8,128,576]{3,2,1,0:T(8,128)(2,1)} %copy.109, s32[2048]{0:T(1024)S(1)} %reshape.256), kind=kCustom, calls=%fused_computation | custom fusion | bytes 4743168 | tf_op jit(solution)/shard_map/vmap(vmap())/gather | solution.py:38
  307.2 2.8 select_reduce_fusion
  310.0 1.1 fusion.3
  311.2 8.8 reshape.249
  320.5 8.7 convolution_convert_fusion
  329.2 15.5 %reshape.250 = bf16[64,1,128,576]{3,2,0,1:T(8,128)(2,1)} reshape(bf16[64,73728]{1,0:T(8,128)(2,1)} %convolution_convert_fusion) | data formatting | bytes 18874368 | tf_op jit(solution)/shard_map/reshape | solution.py:188
  344.7 13.9 %copy.123 = bf16[64,1,128,576]{2,3,1,0:T(8,128)(2,1)} copy(bf16[64,1,128,576]{3,2,0,1:T(8,128)(2,1)} %reshape.250) | data formatting | bytes 18874368 | tf_op jit(solution)/shard_map/reshape | solution.py:188
  358.6 10.9 %all-to-all-start = ((bf16[64,1,128,576]{2,3,1,0:T(8,128)(2,1)}), bf16[64,1,128,576]{2,3,1,0:T(8,128)(2,1)}, u32[]{:S(2)}, u32[]{:S(2)}) async-start(bf16[64,1,128,576]{2,3,1,0:T(8,128)(2,1)} %copy.123), calls=%async_computation | async-start | bytes 18874368 | tf_op jit(solution)/shard_map/all_to_all | solution.py:187
  371.6 259.4 %all-gather.4 = f32[64,4,12]{2,1,0:T(4,128)S(1)} all-gather(f32[1,4,12]{2,1,0:T(4,128)S(1)} %bitcast.156), channel_id=3, replica_groups=mesh['head'=4,'page'=64] {'page'}, dimensions={0}, use_global_device_ids=true | all-gather | bytes 12480 | tf_op jit(solution)/shard_map/all_gather | solution.py:14
  631.0 47.8 %all-gather.3 = f32[64,4,12]{2,1,0:T(4,128)S(1)} all-gather(f32[1,4,12]{2,1,0:T(4,128)S(1)} %bitcast.154), channel_id=2, replica_groups=mesh['head'=4,'page'=64] {'page'}, dimensions={0}, use_global_device_ids=true | all-gather | bytes 12480 | tf_op jit(solution)/shard_map/all_gather | solution.py:14
  680.5 66.4 %while.19 = (s32[]{:T(128)}, f32[4,12]{1,0:T(4,128)S(1)}, f32[4,12]{1,0:T(4,128)S(1)}, f32[4,12,512]{2,1,0:T(8,128)S(1)}, f32[64,4,12]{2,1,0:T(4,128)S(1)}, /*in...) while((s32[]{:T(128)}, f32[4,12]{1,0:T(4,128)S(1)}, ...), condition=%wide.region_6.7_spmd, body=%wide.region_5.6_spmd.sunk | while | flops 74021 | bytes 296983 | solution.py:19
  680.6 1.0 fusion.118
  681.6 1.0 fusion.118
  682.7 1.0 fusion.118
  683.7 1.0 fusion.118
  684.8 1.0 fusion.118
  685.8 1.0 fusion.118
  686.9 1.0 fusion.118
  689.0 1.0 fusion.118
  691.1 1.0 fusion.118
  693.2 1.0 fusion.118
  695.3 1.0 fusion.118
  697.4 1.0 fusion.118
  698.5 1.0 fusion.118
  699.5 1.0 fusion.118
  700.6 1.0 fusion.118
  701.6 1.0 fusion.118
  702.7 1.0 fusion.118
  703.8 1.0 fusion.118
  704.8 1.0 fusion.118
  705.9 1.0 fusion.118
  706.9 1.0 fusion.118
  709.0 1.0 fusion.118
  711.1 1.0 fusion.118
  713.2 1.0 fusion.118
  746.9 1.3 fusion.23
  748.8 75.9 %psum.22 = bf16[12,2048]{1,0:T(8,128)(2,1)S(1)} all-reduce(f32[12,2048]{1,0:T(8,128)S(1)} %dynamic_update_slice.3), channel_id=1, replica_groups=mesh['head'=4,'page'=64] {'head','page'}, use_global_device_ids=true, to_apply=%region_7.8 | all-reduce | flops 24576 | bytes 147456 | tf_op jit(solution)/shard_map/psum | solution.py:124
  825.1 1.7 gather_fusion.1
  827.9 2.5 convolution_multiply_fusion
  830.4 73.9 %psum.23 = bf16[12,2048]{1,0:T(8,128)(2,1)} all-reduce(f32[12,2048]{1,0:T(8,128)S(1)} %convolution_multiply_fusion), channel_id=1, replica_groups=mesh['head'=4,'page'=64] {'head','page'}, use_global_device_ids=true, to_apply=%region_11.12 | all-reduce | flops 24576 | bytes 147456 | tf_op jit(solution)/shard_map/psum | solution.py:146
  904.3 14.1 %copy.124 = bf16[64,1,128,576]{3,2,0,1:T(8,128)(2,1)} copy(bf16[64,1,128,576]{2,3,1,0:T(8,128)(2,1)} %all-to-all-done) | data formatting | bytes 18874368 | tf_op jit(solution)/shard_map/all_to_all | solution.py:187
  918.4 15.3 %reshape.251 = bf16[64,73728]{1,0:T(8,128)(2,1)} reshape(bf16[64,1,128,576]{3,2,0,1:T(8,128)(2,1)} %copy.124) | data formatting | bytes 18874368 | tf_op jit(solution)/shard_map/reshape | solution.py:196
  933.6 8.0 convolution_convert_fusion.1
  941.7 8.8 reshape.252
  950.5 37.5 %gather_fusion.2 = bf16[2048,576]{1,0:T(8,128)(2,1)} fusion(bf16[32,128,576]{2,1,0:T(8,128)(2,1)} %reshape.252, s32[2048]{0:T(1024)S(1)} %reshape.268), kind=kCustom, calls=%fused_computation.2 | custom fusion | bytes 4734976 | tf_op jit(solution)/shard_map/vmap()/gather | solution.py:38
  (208 shorter events, 48.6 us)
Async XLA Ops:
  7.2 820.7 %copy-start = (bf16[1,352,2048]{2,1,0:T(8,128)(2,1)S(1)}, bf16[1,352,2048]{2,1,0:T(8,128)(2,1)}, u32[]{:S(2)}) copy-start(bf16[1,352,2048]{2,1,0:T(8,128)(2,1)} %param.35) | copy-start | bytes 4325380
  7.2 672.4 %all-gather.7.cloned.1.call-start = ((), (), s32[]{:S(2)}) async-start(), calls=%async_computation.1 | async-start | bytes 8519680 | tf_op jit(solution)/shard_map/all_gather | solution.py:14
  8.5 7.8 copy-start.8
  8.5 7.8 copy-start.11
  8.5 257.7 %copy-start.15 = (s32[12]{0:T(128)S(1)}, s32[12]{0:T(128)}, u32[]{:S(2)}) copy-start(s32[12]{0:T(128)} %param.26) | copy-start | bytes 148
  8.5 257.9 %copy-start.13 = (s32[4,8]{1,0:T(4,128)S(1)}, s32[4,8]{1,0:T(4,128)}, u32[]{:S(2)}) copy-start(s32[4,8]{1,0:T(4,128)} %param.25) | copy-start | bytes 388
  8.5 258.3 %copy-start.6 = (bf16[4,512,64]{1,2,0:T(8,128)(2,1)S(1)}, bf16[4,512,64]{1,2,0:T(8,128)(2,1)}, u32[]{:S(2)}) copy-start(bf16[4,512,64]{1,2,0:T(8,128)(2,1)} %param.28) | copy-start | bytes 786436
  267.1 39.8 %copy-start.5 = (bf16[4,128,512]{2,1,0:T(8,128)(2,1)S(1)}, bf16[4,128,512]{2,1,0:T(8,128)(2,1)}, u32[]{:S(2)}) copy-start(bf16[4,128,512]{2,1,0:T(8,128)(2,1)} %param.21) | copy-start | bytes 1572868
  306.8 3.2 copy-start.1
  311.2 8.8 copy-start.7
  358.6 10.9 %copy-start.12 = (bf16[2048]{0:T(1024)(128)(2,1)S(1)}, bf16[2048]{0:T(1024)(128)(2,1)}, u32[]{:S(2)}) copy-start(bf16[2048]{0:T(1024)(128)(2,1)} %param.30) | copy-start | bytes 12292
  358.6 10.9 %copy-start.9 = (s32[12,6]{0,1:T(8,128)S(1)}, s32[12,6]{0,1:T(8,128)}, u32[]{:S(2)}) copy-start(s32[12,6]{0,1:T(8,128)} %param.32) | copy-start | bytes 868
  358.6 12.2 %copy-start.4 = (s32[4,512,64]{1,2,0:T(8,128)S(1)}, s32[4,512,64]{1,2,0:T(8,128)}, u32[]{:S(2)}) copy-start(s32[4,512,64]{1,2,0:T(8,128)} %param.27) | copy-start | bytes 1572868
  358.6 545.7 %all-to-all-start = ((bf16[64,1,128,576]{2,3,1,0:T(8,128)(2,1)}), bf16[64,1,128,576]{2,3,1,0:T(8,128)(2,1)}, u32[]{:S(2)}, u32[]{:S(2)}) async-start(bf16[64,1,128,576]{2,3,1,0:T(8,128)(2,1)} %copy.123), calls=%async_computation | async-start | bytes 18874368 | tf_op jit(solution)/shard_map/all_to_all | solution.py:187
  370.8 377.4 %copy-start.10 = (bf16[512,32]{0,1:T(8,128)(2,1)S(1)}, bf16[512,32]{0,1:T(8,128)(2,1)}, u32[]{:S(2)}) copy-start(bf16[512,32]{0,1:T(8,128)(2,1)} %param.23) | copy-start | bytes 98308
  371.4 453.5 %copy-start.14 = (bf16[2048,64]{0,1:T(8,128)(2,1)S(1)}, bf16[2048,64]{0,1:T(8,128)(2,1)}, u32[]{:S(2)}) copy-start(bf16[2048,64]{0,1:T(8,128)(2,1)} %param.31) | copy-start | bytes 786436
  824.7 3.2 copy-start.3
  825.1 2.3 copy-start.2
Sparse Core Ops, SparseCore 0:
  311.3 121.7 all-gather.6
where the time goes:
time: 999 us; the launch traced here: 995 us
  blocking collectives  707 us (71%)
  local copies, waits for them, and re-layouts  168 us (17%)
  other arithmetic  66.3 us (7%)
  matrix products  26.8 us (3%)
  between operations  14.4 us (1%)
  starting transfers between devices  10.9 us (1%)
    all_gather x2, blocking collectives, joined_2(): gathered = jax.tree.map(lambda a: lax.all_gather(a, axis), part)  307 us
    psum x1, blocking collectives, shards(): lax.psum(partial_value, 'page').reshape(requests, heads_here, head_size)  250 us
    gather x4, local copies, waits for them, and re-layouts, pick_rows(): return one_page[row_ids]  77.4 us
    psum x1, blocking collectives, shards(): attn_out = lax.psum(padded, ('head', 'page')).astype(jnp.bfloat16)  75.9 us
    psum x1, blocking collectives, shards(): moe_out = lax.psum(expert_terms, ('head', 'page')).astype(jnp.bfloat16)  73.9 us
    add x63, other arithmetic, merge_parts(): left_part[2] * left_factor[..., None]  62.9 us
    reshape x2, local copies, waits for them, and re-layouts, shards(): outgoing.reshape(groups, sending_limit, page_rows, latent_dim)  29.4 us
  transfers between devices with their start and end apart: 2, of which 0 were waited for; matrix products, arithmetic and copies ran while one was open for 12% of the time, Pallas kernels for 0%

commit v1 on v0

--- a/solution.py
+++ b/solution.py
@@ -82,7 +82,9 @@
     sending_limit = (blocks + groups - 1) // groups
     first_page = page_index * pages_here
     partial_value = jnp.dot(hidden, q_weight, preferred_element_type=jnp.float32)
-    queries = lax.psum(partial_value, "page").reshape(requests, heads_here, head_size)
+    queries = jnp.sum(lax.all_gather(partial_value, "page"), axis=0).reshape(
+        requests, heads_here, head_size
+    )
     q_nope = queries[..., :QK_NOPE].astype(jnp.bfloat16)
     positions = seq_pages * page_rows - 1
     q_rope = rotate_query(queries[..., QK_NOPE:], positions).astype(jnp.bfloat16)

time: 999 us -> 785 us (0.79)
  blocking collectives: 707 us -> 458 us
  waiting for transfers between devices: 0.02 us -> 35.5 us
    psum x1 -> x0, blocking collectives: 250 us -> none  [shards(): lax.psum(partial_value, 'page').reshape(requests, heads_here, head_size)]
    all_gather x0 -> x1, waiting for transfers between devices: none -> 35.4 us  [shards(): lax.all_gather(partial_value, 'page')]
  transfers between devices with their start and end apart: 2 -> 3, of which waited for: 0 -> 1; matrix products, arithmetic and copies ran while one was open for 12% -> 22% of each run, Pallas kernels for 0% -> 0%
where the time goes in v1:
time: 785 us; the launch traced here: 781 us
  blocking collectives  458 us (58%)
  local copies, waits for them, and re-layouts  168 us (21%)
  other arithmetic  68.2 us (9%)
  waiting for transfers between devices  35.5 us (5%)
  matrix products  28.3 us (4%)
  between operations  14.4 us (2%)
    all_gather x2, blocking collectives, joined_2(): gathered = jax.tree.map(lambda a: lax.all_gather(a, axis), part)  308 us
    gather x4, local copies, waits for them, and re-layouts, pick_rows(): return one_page[row_ids]  77.4 us
    psum x1, blocking collectives, shards(): attn_out = lax.psum(padded, ('head', 'page')).astype(jnp.bfloat16)  76.1 us
    psum x1, blocking collectives, shards(): moe_out = lax.psum(expert_terms, ('head', 'page')).astype(jnp.bfloat16)  74 us
    add x63, other arithmetic, merge_parts(): left_part[2] * left_factor[..., None]  62.9 us
    all_gather x1, waiting for transfers between devices, shards(): lax.all_gather(partial_value, 'page')  35.4 us
    reshape x2, local copies, waits for them, and re-layouts, shards(): outgoing.reshape(groups, sending_limit, page_rows, latent_dim)  29.4 us
  transfers between devices with their start and end apart: 3, of which 1 were waited for; matrix products, arithmetic and copies ran while one was open for 22% of the time, Pallas kernels for 0%

profile of v1, /device:TPU:1, one launch (start us, length us, event | category | flops | bytes accessed | tf_op | source)
XLA Modules:
  0.0 781.2 jit_solution(14526703988807643904)
XLA Ops:
  7.2 1.7 convolution_bitcast_fusion
  9.0 1.0 constant_dynamic-slice_fusion.2
  10.2 7.7 copy.117
  18.7 39.7 %gather_fusion = bf16[2048,576]{1,0:T(8,128)(2,1)} fusion(bf16[4,8,128,576]{3,2,1,0:T(8,128)(2,1)} %copy.117, s32[2048]{0:T(1024)S(1)} %reshape.256), kind=kCustom, calls=%fused_computation | custom fusion | bytes 4743168 | tf_op jit(solution)/shard_map/vmap(vmap())/gather | solution.py:38
  58.6 35.4 %all-gather.12.cloned.1.call-done = f32[64,12,768]{2,1,0:T(8,128)} async-done(((f32[1,12,768]{2,1,0:T(8,128)}), f32[64,12,768]{2,1,0:T(8,128)}) %all-gather.12.cloned.1.call-update) | async-done | bytes 2359312 | tf_op jit(solution)/shard_map/all_gather | solution.py:85
  94.0 2.1 reduce_sum.68
  96.5 2.8 select_reduce_fusion
  99.3 1.1 fusion.3
  100.4 8.8 %reshape.249 = bf16[32,73728]{1,0:T(8,128)(2,1)} reshape(bf16[4,8,128,576]{3,2,1,0:T(8,128)(2,1)} %copy.117) | data formatting | bytes 9437184 | tf_op jit(solution)/shard_map/reshape | solution.py:185
  109.7 8.8 %convolution_convert_fusion = bf16[64,73728]{1,0:T(8,128)(2,1)} fusion(bf16[32,73728]{1,0:T(8,128)(2,1)} %reshape.249, s32[32]{0:T(128)S(1)} %add_add_fusion.1), kind=kOutput, calls=%fused_computation.11 | convolution fusion | flops 306710528 | bytes 14155904 | tf_op jit(solution)/shard_map/bc,bx->cx/dot_general | solution.py:186
  118.4 15.5 %reshape.250 = bf16[64,1,128,576]{3,2,0,1:T(8,128)(2,1)} reshape(bf16[64,73728]{1,0:T(8,128)(2,1)} %convolution_convert_fusion) | data formatting | bytes 18874368 | tf_op jit(solution)/shard_map/reshape | solution.py:190
  133.9 13.9 %copy.131 = bf16[64,1,128,576]{2,3,1,0:T(8,128)(2,1)} copy(bf16[64,1,128,576]{3,2,0,1:T(8,128)(2,1)} %reshape.250) | data formatting | bytes 18874368 | tf_op jit(solution)/shard_map/reshape | solution.py:190
  147.9 6.6 all-to-all-start
  157.4 259.6 %all-gather.6 = f32[64,4,12]{2,1,0:T(4,128)S(1)} all-gather(f32[1,4,12]{2,1,0:T(4,128)S(1)} %bitcast.158), channel_id=4, replica_groups=mesh['head'=4,'page'=64] {'page'}, dimensions={0}, use_global_device_ids=true | all-gather | bytes 12480 | tf_op jit(solution)/shard_map/all_gather | solution.py:14
  417.0 48.7 %all-gather.5 = f32[64,4,12]{2,1,0:T(4,128)S(1)} all-gather(f32[1,4,12]{2,1,0:T(4,128)S(1)} %bitcast.156), channel_id=3, replica_groups=mesh['head'=4,'page'=64] {'page'}, dimensions={0}, use_global_device_ids=true | all-gather | bytes 12480 | tf_op jit(solution)/shard_map/all_gather | solution.py:14
  466.6 66.3 %while.19 = (s32[]{:T(128)}, f32[4,12]{1,0:T(4,128)S(1)}, f32[4,12]{1,0:T(4,128)S(1)}, f32[4,12,512]{2,1,0:T(8,128)S(1)}, f32[64,4,12]{2,1,0:T(4,128)S(1)}, /*in...) while((s32[]{:T(128)}, f32[4,12]{1,0:T(4,128)S(1)}, ...), condition=%wide.region_6.7_spmd, body=%wide.region_5.6_spmd.sunk | while | flops 74021 | bytes 296983 | solution.py:19
  466.7 1.0 fusion.123
  467.7 1.0 fusion.123
  468.8 1.0 fusion.123
  470.9 1.0 fusion.123
  471.9 1.0 fusion.123
  474.0 1.0 fusion.123
  475.1 1.0 fusion.123
  476.1 1.0 fusion.123
  478.3 1.0 fusion.123
  479.3 1.0 fusion.123
  480.4 1.0 fusion.123
  482.5 1.0 fusion.123
  483.5 1.0 fusion.123
  484.6 1.0 fusion.123
  486.7 1.0 fusion.123
  487.7 1.0 fusion.123
  488.8 1.0 fusion.123
  490.9 1.0 fusion.123
  491.9 1.0 fusion.123
  494.0 1.0 fusion.123
  495.1 1.0 fusion.123
  496.1 1.0 fusion.123
  532.9 1.3 fusion.23
  534.7 76.1 %psum.14 = bf16[12,2048]{1,0:T(8,128)(2,1)S(1)} all-reduce(f32[12,2048]{1,0:T(8,128)S(1)} %dynamic_update_slice.3), channel_id=1, replica_groups=mesh['head'=4,'page'=64] {'head','page'}, use_global_device_ids=true, to_apply=%region_7.8 | all-reduce | flops 24576 | bytes 147456 | tf_op jit(solution)/shard_map/psum | solution.py:126
  611.3 1.7 gather_fusion.1
  614.1 2.5 convolution_multiply_fusion
  616.6 74.0 %psum.15 = bf16[12,2048]{1,0:T(8,128)(2,1)} all-reduce(f32[12,2048]{1,0:T(8,128)S(1)} %convolution_multiply_fusion), channel_id=1, replica_groups=mesh['head'=4,'page'=64] {'head','page'}, use_global_device_ids=true, to_apply=%region_11.12 | all-reduce | flops 24576 | bytes 147456 | tf_op jit(solution)/shard_map/psum | solution.py:148
  690.6 14.1 %copy.132 = bf16[64,1,128,576]{3,2,0,1:T(8,128)(2,1)} copy(bf16[64,1,128,576]{2,3,1,0:T(8,128)(2,1)} %all-to-all-done) | data formatting | bytes 18874368 | tf_op jit(solution)/shard_map/all_to_all | solution.py:189
  704.7 15.3 %reshape.251 = bf16[64,73728]{1,0:T(8,128)(2,1)} reshape(bf16[64,1,128,576]{3,2,0,1:T(8,128)(2,1)} %copy.132) | data formatting | bytes 18874368 | tf_op jit(solution)/shard_map/reshape | solution.py:198
  720.0 8.0 %convolution_convert_fusion.1 = bf16[32,73728]{1,0:T(8,128)(2,1)} fusion(bf16[64,73728]{1,0:T(8,128)(2,1)} %reshape.251, s32[64,32]{1,0:T(8,128)S(1)} %add_add_fusion, s32[64,32]{1,0:T(8,128)S(1)} %copy.126, pred[64,32]{1,0:T(8,128)(4,1)S(1)} %copy.128), kind=kOutput, calls=%fused_computation.12 | convolution fusion | flops 313001984 | bytes 14174208 | tf_op jit(solution)/shard_map/dot_general | solution.py:196
  728.0 8.8 %reshape.252 = bf16[32,128,576]{2,1,0:T(8,128)(2,1)} reshape(bf16[32,73728]{1,0:T(8,128)(2,1)} %convolution_convert_fusion.1) | data formatting | bytes 9437184 | tf_op jit(solution)/shard_map/reshape | solution.py:202
  736.8 37.5 %gather_fusion.2 = bf16[2048,576]{1,0:T(8,128)(2,1)} fusion(bf16[32,128,576]{2,1,0:T(8,128)(2,1)} %reshape.252, s32[2048]{0:T(1024)S(1)} %reshape.268), kind=kCustom, calls=%fused_computation.2 | custom fusion | bytes 4734976 | tf_op jit(solution)/shard_map/vmap()/gather | solution.py:38
  (208 shorter events, 50.4 us)
Async XLA Ops:
  7.2 606.9 %copy-start = (bf16[1,352,2048]{2,1,0:T(8,128)(2,1)S(1)}, bf16[1,352,2048]{2,1,0:T(8,128)(2,1)}, u32[]{:S(2)}) copy-start(bf16[1,352,2048]{2,1,0:T(8,128)(2,1)} %param.35) | copy-start | bytes 4325380
  7.2 86.8 %all-gather.12.cloned.1.call-start = ((), (), s32[]{:S(2)}) async-start(), calls=%async_computation.2 | async-start | bytes 3194880 | tf_op jit(solution)/shard_map/all_gather | solution.py:85
  8.9 456.8 %all-gather.10.cloned.1.call-start = ((), (), s32[]{:S(2)}) async-start(), calls=%async_computation.1 | async-start | bytes 8519680 | tf_op jit(solution)/shard_map/all_gather | solution.py:14
  10.2 7.8 copy-start.13
  10.2 7.9 %copy-start.11 = (s32[4,8]{1,0:T(4,128)S(1)}, s32[4,8]{1,0:T(4,128)}, u32[]{:S(2)}) copy-start(s32[4,8]{1,0:T(4,128)} %param.25) | copy-start | bytes 388
  10.2 8.3 %copy-start.6 = (bf16[4,512,64]{1,2,0:T(8,128)(2,1)S(1)}, bf16[4,512,64]{1,2,0:T(8,128)(2,1)}, u32[]{:S(2)}) copy-start(bf16[4,512,64]{1,2,0:T(8,128)(2,1)} %param.28) | copy-start | bytes 786436
  58.4 37.8 %copy-start.5 = (bf16[4,128,512]{2,1,0:T(8,128)(2,1)S(1)}, bf16[4,128,512]{2,1,0:T(8,128)(2,1)}, u32[]{:S(2)}) copy-start(bf16[4,128,512]{2,1,0:T(8,128)(2,1)} %param.21) | copy-start | bytes 1572868
  96.2 3.1 copy-start.1
  100.4 8.8 %copy-start.7 = (s32[4,512]{1,0:T(4,128)S(1)}, s32[4,512]{1,0:T(4,128)}, u32[]{:S(2)}) copy-start(s32[4,512]{1,0:T(4,128)} %param.29) | copy-start | bytes 24580
  147.8 6.6 copy-start.10
  147.8 6.7 copy-start.8
  147.8 7.9 %copy-start.4 = (s32[4,512,64]{1,2,0:T(8,128)S(1)}, s32[4,512,64]{1,2,0:T(8,128)}, u32[]{:S(2)}) copy-start(s32[4,512,64]{1,2,0:T(8,128)} %param.27) | copy-start | bytes 1572868
  147.9 542.7 %all-to-all-start = ((bf16[64,1,128,576]{2,3,1,0:T(8,128)(2,1)}), bf16[64,1,128,576]{2,3,1,0:T(8,128)(2,1)}, u32[]{:S(2)}, u32[]{:S(2)}) async-start(bf16[64,1,128,576]{2,3,1,0:T(8,128)(2,1)} %copy.131), calls=%async_computation | async-start | bytes 18874368 | tf_op jit(solution)/shard_map/all_to_all | solution.py:189
  155.8 378.4 %copy-start.9 = (bf16[512,32]{0,1:T(8,128)(2,1)S(1)}, bf16[512,32]{0,1:T(8,128)(2,1)}, u32[]{:S(2)}) copy-start(bf16[512,32]{0,1:T(8,128)(2,1)} %param.23) | copy-start | bytes 98308
  156.4 454.7 %copy-start.12 = (bf16[2048,64]{0,1:T(8,128)(2,1)S(1)}, bf16[2048,64]{0,1:T(8,128)(2,1)}, u32[]{:S(2)}) copy-start(bf16[2048,64]{0,1:T(8,128)(2,1)} %param.31) | copy-start | bytes 786436
  610.9 3.2 copy-start.3
  611.3 2.3 copy-start.2
Sparse Core Ops, SparseCore 0:
  11.3 82.5 all-gather.11
  100.5 121.1 all-gather.9
